TPU v7x, 256 devices: a whole 4x4x8 slice. The times are simulated.
256 devices in a mesh: lat: 4 (over x), lon: 2 (over core), ens: 32 (over z, y).
Axes of the slice: x: 4, y: 4, z: 8, core: 2. Of those that a mesh axis runs over, the one named last changes fastest.
Arguments:
- inputs: bfloat16 [32, 8, 1440, 256], P('ens', 'lat', 'lon'), may hold values from -12 to 12
- weight: bfloat16 [9, 256, 256], replicated, may hold values from -0.125 to 0.125
- spread: int32 [8], P('lat'), may hold values from 2 to 16, as said below
- target: bfloat16 [8, 1440, 256], P('lat', 'lon'), may hold values from -6 to 6
Outputs:
- response: bfloat16 [32, 8, 1440, 256], P('ens', 'lat', 'lon')
- grad_input: bfloat16 [32, 8, 1440, 256], P('ens', 'lat', 'lon')
- grad_weight: float32 [9, 256, 256], replicated
- loss: float32 [], replicated
Inputs may be any that keep to these rules, and one draw needn't show every extreme that they name: The filter of row o spans 2 spread[o] + 1 longitudes; spread is 16 on the 2 polar rows at each pole, which ignore it, and on the next row toward the equator.
All inputs are finite; a program needn't handle non-finite values.
Results may differ from a plain program's by a relative error of at most 0.009.
Values may be sent and summed in bfloat16 or wider, within the bound.
No kernel may reach another device: no remote copies, remote signals or barrier semaphores. Data moves between devices by JAX's collectives and lax.ppermute only.
A program may use at most 128 MiB of HBM per device.

v0:
```python
import math
import jax
import jax.numpy as jnp
from jax import lax
from jax.sharding import PartitionSpec as P

PCAP = 2
HMAX = 16
highest = lax.Precision.HIGHEST


def extended_2(block, sides, width):
    for axis, dim in sides:
        count = lax.axis_size(axis)
        forward = [(i, i + 1) for i in range(count - 1)]
        backward = [(target, source) for source, target in forward]
        low = lax.ppermute(
            lax.slice_in_dim(block, block.shape[dim] - width, None, axis=dim), axis, forward
        )
        high = lax.ppermute(lax.slice_in_dim(block, 0, width, axis=dim), axis, backward)
        block = jnp.concatenate([low, block, high], axis=dim)
    return block


def kernel_rows(spread_rows, lon_count, reach):
    halves = spread_rows.astype(jnp.float32)[:, None, None, None] / 2.0
    columns = jnp.arange(lon_count)
    window_cols = jnp.arange(lon_count + 2 * reach)
    offsets = (window_cols[None, :] - reach - columns[:, None]).astype(jnp.float32)
    centres = (jnp.arange(3) - 1).astype(jnp.float32)[None, :, None, None] * halves
    values = jnp.maximum(0.0, 1.0 - jnp.abs(offsets[None, None] - centres) / halves) / halves
    return values.astype(jnp.bfloat16)


def circle_basis(first_col, lon_count, circle):
    angles = 2.0 * math.pi * (first_col + jnp.arange(lon_count)).astype(jnp.float32) / circle
    return jnp.stack([jnp.ones_like(angles), jnp.cos(angles), jnp.sin(angles)])


def circular(circle_sums, basis, circle, row_count):
    cos_wave = basis[1][None, None, :, None]
    sin_wave = basis[2][None, None, :, None]
    pieces = []
    for lat_tap in range(3):
        tap_sums = circle_sums[:, :, lat_tap : lat_tap + row_count]
        mean_part = tap_sums[:, 0][:, :, None, :] / circle
        cosine_part = (
            2.0
            / circle
            * (cos_wave * tap_sums[:, 1][:, :, None, :] + sin_wave * tap_sums[:, 2][:, :, None, :])
        )
        sine_part = (
            2.0
            / circle
            * (cos_wave * tap_sums[:, 2][:, :, None, :] - sin_wave * tap_sums[:, 1][:, :, None, :])
        )
        pieces += [jnp.broadcast_to(mean_part, cosine_part.shape), cosine_part, sine_part]
    return jnp.stack(pieces, 2)


def crps_terms(values, every_member, truth, lat_weight, member_total):
    miss = values - truth
    own_dist = jnp.sqrt(miss * miss + 0.25)
    own_slope = miss / own_dist

    def add_member(member, carry):
        pair_dist, pair_slope = carry
        other = lax.dynamic_index_in_dim(every_member, member, 0, keepdims=True).astype(jnp.float32)
        gap_value = values - other
        distance = jnp.sqrt(gap_value * gap_value + 0.25)
        return (pair_dist + distance, pair_slope + gap_value / distance)

    start = (jnp.zeros_like(values), jnp.zeros_like(values))
    pair_dist, pair_slope = lax.fori_loop(0, member_total, add_member, start)
    pair_dist = pair_dist - 0.5
    scores = own_dist / member_total - pair_dist / (2 * member_total * (member_total - 1))
    weighted = jnp.sum(lat_weight * scores)
    slopes = (
        lat_weight * (own_slope / member_total - pair_slope / (member_total * (member_total - 1)))
    ).astype(jnp.bfloat16)
    return (weighted, slopes)


def per_device(inputs, weight, spread, target):
    ens_local, row_count, lon_count, channels = inputs.shape
    reach = HMAX
    lat_total = row_count * lax.axis_size("lat")
    lon_total = lon_count * lax.axis_size("lon")
    lon_first = lax.axis_index("lon") * lon_count
    global_rows = lax.axis_index("lat") * row_count + jnp.arange(row_count)
    polar_rows = (global_rows < PCAP) | (global_rows >= lat_total - PCAP)
    polar_mask = polar_rows[None, :, None, None, None]
    kernels = kernel_rows(spread, lon_count, reach)
    local_basis = circle_basis(lon_first, lon_count, lon_total)
    extended = extended_2(inputs, (("lat", 1),), 1)
    whole_circle = lax.all_gather(extended, "lon", axis=2, tiled=True)
    window_start = (lon_first - reach + lon_total) % lon_total
    doubled = jnp.concatenate([whole_circle, whole_circle], 2)
    window = lax.dynamic_slice_in_dim(doubled, window_start, lon_count + 2 * reach, 2)
    full_basis = circle_basis(0, lon_total, lon_total)
    circle_sums = jnp.einsum(
        "pj,erjc->eprc", full_basis, whole_circle.astype(jnp.float32), precision=highest
    )
    banded = jnp.concatenate(
        [
            jnp.einsum(
                "objq,eoqc->eobjc",
                kernels,
                window[:, lat_tap : lat_tap + row_count],
                preferred_element_type=jnp.float32,
            )
            for lat_tap in range(3)
        ],
        2,
    )
    rounds = circular(circle_sums, local_basis, lon_total, row_count)
    features = jnp.where(polar_mask, rounds, banded).astype(jnp.bfloat16)
    response = jnp.einsum(
        "eokjc,kcd->eojd", features, weight, preferred_element_type=jnp.float32
    ).astype(jnp.bfloat16)
    member_total = ens_local * lax.axis_size("ens")
    row_weight = jnp.sin(math.pi * (global_rows.astype(jnp.float32) + 0.5) / lat_total)
    ensemble = lax.all_gather(response, "ens", axis=0, tiled=True)
    truth = target.astype(jnp.float32)[None]
    weighted, slopes = crps_terms(
        response.astype(jnp.float32), ensemble, truth, row_weight[None, :, None, None], member_total
    )
    loss_part = weighted / (lat_total * lon_total * channels)
    weight_part = jnp.einsum(
        "eokjc,eojd->kcd", features, slopes, preferred_element_type=jnp.float32
    )
    weight_sum, loss = lax.psum((weight_part, loss_part), ("lat", "lon", "ens"))
    grad_weight = weight_sum * math.sqrt(weight.shape[0] * channels) / (lat_total * lon_total)
    feature_grad = jnp.einsum(
        "eojd,kcd->eokjc", slopes, weight, preferred_element_type=jnp.float32
    ).astype(jnp.bfloat16)
    zero_grad = jnp.zeros_like(feature_grad)
    band_grad = jnp.where(polar_mask, zero_grad, feature_grad)
    circle_grad = jnp.where(polar_mask, feature_grad, zero_grad)
    window_grad = jnp.zeros(
        (ens_local, row_count + 2, lon_count + 2 * reach, channels), jnp.float32
    )
    sum_grad = jnp.zeros((ens_local, 3, row_count + 2, channels), jnp.float32)
    cos_wave = local_basis[1]
    sin_wave = local_basis[2]
    for lat_tap in range(3):
        picked = band_grad[:, :, 3 * lat_tap : 3 * lat_tap + 3]
        window_grad = window_grad.at[:, lat_tap : lat_tap + row_count].add(
            jnp.einsum("objq,eobjc->eoqc", kernels, picked, preferred_element_type=jnp.float32)
        )
        tap_grad = circle_grad[:, :, 3 * lat_tap : 3 * lat_tap + 3].astype(jnp.float32)
        mean_grad = jnp.sum(tap_grad[:, :, 0], axis=2) / lon_total
        cos_grad = (
            2.0
            / lon_total
            * (
                jnp.einsum("j,eojc->eoc", cos_wave, tap_grad[:, :, 1], precision=highest)
                - jnp.einsum("j,eojc->eoc", sin_wave, tap_grad[:, :, 2], precision=highest)
            )
        )
        sin_grad = (
            2.0
            / lon_total
            * (
                jnp.einsum("j,eojc->eoc", sin_wave, tap_grad[:, :, 1], precision=highest)
                + jnp.einsum("j,eojc->eoc", cos_wave, tap_grad[:, :, 2], precision=highest)
            )
        )
        sum_grad = sum_grad.at[:, :, lat_tap : lat_tap + row_count].add(
            jnp.stack([mean_grad, cos_grad, sin_grad], 1)
        )
    spread_back = jnp.einsum("pj,eprc->erjc", full_basis, sum_grad, precision=highest)
    placed = jnp.zeros((ens_local, row_count + 2, 2 * lon_total, channels), jnp.float32)
    placed = lax.dynamic_update_slice_in_dim(placed, window_grad, window_start, 2)
    spread_back = spread_back + placed[:, :, :lon_total] + placed[:, :, lon_total:]
    core = lax.psum_scatter(
        spread_back.astype(jnp.bfloat16), "lon", scatter_dimension=2, tiled=True
    ).astype(jnp.float32)
    edges = jnp.concatenate([core[:, :1], core[:, row_count + 1 :]], 1)
    arrived_rows = extended_2(edges.astype(jnp.bfloat16), (("lat", 1),), 1).astype(edges.dtype)
    inner = core[:, 1 : row_count + 1]
    inner = inner.at[:, 0].add(arrived_rows[:, 0])
    inner = inner.at[:, row_count - 1].add(arrived_rows[:, 3])
    return (response, inner.astype(jnp.bfloat16), grad_weight, loss)


def solution(mesh):
    in_specs = (P("ens", "lat", "lon", None), P(), P("lat"), P("lat", "lon", None))
    out_specs = (P("ens", "lat", "lon", None), P("ens", "lat", "lon", None), P(), P())
    return jax.shard_map(
        per_device, mesh=mesh, in_specs=in_specs, out_specs=out_specs, check_vma=False
    )
```

profile of v0, /device:TPU:2, one launch (start us, length us, event | category | flops | bytes accessed | tf_op | source)
XLA Modules:
  0.0 740.7 jit_solution(5865980801284775677)
XLA Ops:
  8.5 3.4 collective-permute-start
  14.4 6.3 collective-permute-done
  27.0 19.3 %all-gather.4.cloned.1.call-done = bf16[1,4,1440,256]{3,2,1,0:T(8,128)(2,1)} async-done(((bf16[1,4,720,256]{3,2,1,0:T(8,128)(2,1)}), bf16[1,4,1440,256]{3,2,1,0:T(8,128)(2,1)}) %all-gather.4.cloned.1.call-update) | async-done | bytes 2949136 | tf_op jit(solution)/shard_map/all_gather | solution.py:96
  71.5 174.4 %all-gather.6.cloned.1.call-done = bf16[64,720,256]{2,1,0:T(8,128)(2,1)} async-done(((bf16[2,720,256]{2,1,0:T(8,128)(2,1)}), bf16[64,720,256]{2,1,0:T(8,128)(2,1)}) %all-gather.6.cloned.1.call-update) | async-done | bytes 23592976 | tf_op jit(solution)/shard_map/all_gather | solution.py:123
  245.9 140.6 %while.24 = (s32[]{:T(128)}, f32[1,2,720,256]{3,2,1,0:T(8,128)}, f32[1,2,720,256]{3,2,1,0:T(8,128)}, bf16[32,2,720,256]{3,2,1,0:T(8,128)(2,1)}, f32[1,2,720,256]{3,2,1,0:T(8,128)S(1)}, /*index=5*/s32[]{:T(128)}, s32[]{:T(128)}) while((s32[]{:T(128)}, f32[1,2,720,256]{3,2,1,0:T(8,128)}, f32[1,2,720,256]{3,2,1,0:T(8,128)}, ...), condition=%wide.region_1.2_spmd.clone, body=%wide.region_0.1_spmd.clone.sunk | while | flops 3317763 | bytes 8110179 | solution.py:74
  245.9 3.6 select_add_fusion.3
  249.5 4.4 select_add_fusion.3
  253.9 4.4 select_add_fusion.3
  258.3 4.4 select_add_fusion.3
  262.7 4.4 select_add_fusion.3
  267.2 4.4 select_add_fusion.3
  271.6 4.4 select_add_fusion.3
  276.0 4.4 select_add_fusion.3
  280.4 4.4 select_add_fusion.3
  284.8 4.4 select_add_fusion.3
  289.3 4.4 select_add_fusion.3
  293.7 4.4 select_add_fusion.3
  298.1 4.4 select_add_fusion.3
  302.5 4.4 select_add_fusion.3
  306.9 4.4 select_add_fusion.3
  311.4 4.4 select_add_fusion.3
  315.8 4.4 select_add_fusion.3
  320.2 4.4 select_add_fusion.3
  324.6 4.4 select_add_fusion.3
  329.0 4.4 select_add_fusion.3
  333.5 4.4 select_add_fusion.3
  337.9 4.4 select_add_fusion.3
  342.3 4.4 select_add_fusion.3
  346.7 4.4 select_add_fusion.3
  351.2 4.4 select_add_fusion.3
  355.6 4.4 select_add_fusion.3
  360.0 4.4 select_add_fusion.3
  364.4 4.4 select_add_fusion.3
  368.8 4.4 select_add_fusion.3
  373.3 4.4 select_add_fusion.3
  377.7 4.4 select_add_fusion.3
  382.1 4.4 select_add_fusion.3
  386.5 3.9 fusion.14
  390.4 3.9 fusion.1
  399.8 5.7 fusion.12
  407.4 6.8 fusion.11
  414.2 6.8 fusion.10
  420.9 5.4 broadcast_in_dim.38
  426.3 8.8 %dynamic_update_slice.3 = f32[1,4,2880,256]{3,2,1,0:T(8,128)} dynamic-update-slice(f32[1,4,2880,256]{3,2,1,0:T(8,128)} %broadcast_in_dim.38, f32[1,4,752,256]{3,2,1,0:T(8,128)} %fusion.10, s32[]{:T(128)} %constant.322.clone.1, s32[]{:T(128)} %constant.322.clone.1, s32[]{:T(128)S(6)} %select_n.39, s32[]{:T(128)} %constant.322.clone.1) | dynamic-update-slice | bytes 6160388 | tf_op jit(solution)/shard_map/dynamic_update_slice | solution.py:174
  435.2 9.4 %fusion.3 = bf16[1,4,1440,256]{3,2,1,0:T(8,128)(2,1)} fusion(f32[1,4,2880,256]{3,2,1,0:T(8,128)} %dynamic_update_slice.3, f32[3,4,256]{2,0,1:T(4,128)S(1)} %fusion.41, f32[1,1440]{1,0:T(1,128)S(1)} %copy-done.11, f32[1,1440]{1,0:T(1,128)S(1)} %copy-done.13, f32[3]{0:T(128)S(1)} %copy-done.15), kind=kOutput, calls=%fused_computation.12 | convolution fusion | flops 57516480 | bytes 14769420 | tf_op jit(solution)/shard_map/pj,eprc->erjc/dot_general | solution.py:172
  445.7 6.4 convolution_bitcast_fusion.3
  452.8 73.8 %psum.15 = f32[]{:T(128)} all-reduce(f32[]{:T(128)S(6)} %div.141), channel_id=1, replica_groups=mesh['lat'=4,'lon'=2,'ens'=32] {'lat','lon','ens'}, use_global_device_ids=true, to_apply=%region_8.9 | all-reduce | flops 1 | bytes 8 | tf_op jit(solution)/shard_map/psum | solution.py:132
  533.8 195.4 %all-reduce.4.cloned.1.call-done = f32[9,256,256]{2,1,0:T(8,128)} async-done(((f32[9,256,256]{2,1,0:T(8,128)}), f32[9,256,256]{2,1,0:T(8,128)}) %all-reduce.4.cloned.1.call-update) | async-done | bytes 2359312 | tf_op jit(solution)/shard_map/psum | solution.py:132
  (133 shorter events, 55.3 us)
Async XLA Ops:
  7.2 60.0 %copy-start = (bf16[9,256,256]{2,1,0:T(8,128)(2,1)S(1)}, bf16[9,256,256]{2,1,0:T(8,128)(2,1)}, u32[]{:S(2)}) copy-start(bf16[9,256,256]{2,1,0:T(8,128)(2,1)} %param.23) | copy-start | bytes 3538948
  7.2 19.3 %copy-start.16 = (s32[2]{0:T(128)S(1)}, s32[2]{0:T(128)}, u32[]{:S(2)}) copy-start(s32[2]{0:T(128)} %param.24) | copy-start | bytes 28
  7.2 39.1 %all-gather.4.cloned.1.call-start = ((), (), s32[]{:S(2)}) async-start(), calls=%async_computation.1 | async-start | bytes 4423680 | tf_op jit(solution)/shard_map/all_gather | solution.py:96
  8.5 12.2 %collective-permute-start = (bf16[1,1,720,256]{3,2,1,0:T(8,128)(2,1)S(1)}, bf16[1,1,720,256]{3,2,1,0:T(8,128)(2,1)S(1)}, u32[]{:S(2)}, u32[]{:S(2)}) collective-permute-start(bf16[1,1,720,256]{3,2,1,0:T(8,128)(2,1)S(1)} %get-tuple-element.236), channel_id=1, source_target_pairs={{0,64},{64,128},{128,192},{1,65},{65,129},{129,193},{2,66},{66,130... | collective-permute-start | bytes 1105928 | tf_op jit(solution)/shard_map/ppermute | solution.py:17
  11.9 11.9 %collective-permute-start.1 = (bf16[1,1,720,256]{3,2,1,0:T(8,128)(2,1)S(1)}, bf16[1,1,720,256]{3,2,1,0:T(8,128)(2,1)S(1)}, u32[]{:S(2)}, u32[]{:S(2)}) collective-permute-start(bf16[1,1,720,256]{3,2,1,0:T(8,128)(2,1)S(1)} %get-tuple-element.237), channel_id=1, source_target_pairs={{64,0},{128,64},{192,128},{65,1},{129,65},{193,129},{66,2},{130,66... | collective-permute-start | bytes 1105928 | tf_op jit(solution)/shard_map/ppermute | solution.py:20
  26.3 219.6 %all-gather.6.cloned.1.call-start = ((), (), s32[]{:S(2)}) async-start(), calls=%async_computation.4 | async-start | bytes 24330240 | tf_op jit(solution)/shard_map/all_gather | solution.py:123
  26.4 25.0 %copy-start.14 = (f32[3]{0:T(128)}, f32[3]{0:T(128)S(1)}, u32[]{:S(2)}) copy-start(f32[3]{0:T(128)S(1)} %pad.37.clone) | copy-start | bytes 40
  26.7 24.6 %copy-start.10 = (f32[1,1440]{1,0:T(1,128)}, f32[1,1440]{1,0:T(1,128)S(1)}, u32[]{:S(2)}) copy-start(f32[1,1440]{1,0:T(1,128)S(1)} %get-tuple-element.247) | copy-start | bytes 17284
  26.7 24.6 %copy-start.12 = (f32[1,1440]{1,0:T(1,128)}, f32[1,1440]{1,0:T(1,128)S(1)}, u32[]{:S(2)}) copy-start(f32[1,1440]{1,0:T(1,128)S(1)} %get-tuple-element.248) | copy-start | bytes 17284
  27.0 30.9 %copy-start.6 = (f32[720,752]{1,0:T(8,128)}, f32[720,752]{1,0:T(8,128)S(1)}, u32[]{:S(2)}) copy-start(f32[720,752]{1,0:T(8,128)S(1)} %subtract_convert_fusion) | copy-start | bytes 6497284
  46.2 3.3 copy-start.2
  64.3 2.8 copy-start.4
  69.9 456.7 %reduce-scatter.2.cloned.1.call-start = ((), (), s32[]{:S(2)}) async-start(), calls=%async_computation.2 | async-start | bytes 4423680 | tf_op jit(solution)/shard_map/reduce_scatter | solution.py:176
  245.9 140.6 %copy-start.5 = (bf16[2,720,256]{2,1,0:T(8,128)(2,1)S(1)}, bf16[2,720,256]{2,1,0:T(8,128)(2,1)}, u32[]{:S(2)}) copy-start(bf16[2,720,256]{2,1,0:T(8,128)(2,1)} %bitcast_convert_fusion) | copy-start | bytes 2211844
  390.4 3.9 copy-start.8
  397.1 2.7 copy-start.7
  426.3 8.8 %copy-start.11 = (f32[1,1440]{1,0:T(1,128)S(1)}, f32[1,1440]{1,0:T(1,128)}, u32[]{:S(2)}) copy-start(f32[1,1440]{1,0:T(1,128)} %copy-done.10) | copy-start | bytes 17284
  426.3 8.8 %copy-start.13 = (f32[1,1440]{1,0:T(1,128)S(1)}, f32[1,1440]{1,0:T(1,128)}, u32[]{:S(2)}) copy-start(f32[1,1440]{1,0:T(1,128)} %copy-done.12) | copy-start | bytes 17284
  426.3 8.8 %copy-start.15 = (f32[3]{0:T(128)S(1)}, f32[3]{0:T(128)}, u32[]{:S(2)}) copy-start(f32[3]{0:T(128)} %copy-done.14) | copy-start | bytes 40
  444.6 1.1 copy-start.9
  444.6 284.5 %all-reduce.4.cloned.1.call-start = ((), (), s32[]{:S(2)}) async-start(), calls=%async_computation.3 | async-start | bytes 4718592 | tf_op jit(solution)/shard_map/psum | solution.py:132
  526.6 205.8 %copy-start.3 = (bf16[1,4,720,256]{3,2,1,0:T(8,128)(2,1)S(1)}, bf16[1,4,720,256]{3,2,1,0:T(8,128)(2,1)}, u32[]{:S(2)}) copy-start(bf16[1,4,720,256]{3,2,1,0:T(8,128)(2,1)} %reduce-scatter.2.cloned.1.call-done) | copy-start | bytes 4423684
  527.9 205.0 %collective-permute-start.2 = (bf16[1,1,720,256]{3,2,1,0:T(8,128)(2,1)S(1)}, bf16[1,1,720,256]{3,2,1,0:T(8,128)(2,1)S(1)}, u32[]{:S(2)}, u32[]{:S(2)}) collective-permute-start(bf16[1,1,720,256]{3,2,1,0:T(8,128)(2,1)S(1)} %get-tuple-element.234), channel_id=1, source_target_pairs={{0,64},{64,128},{128,192},{1,65},{65,129},{129,193},{2,66},{66,130... | collective-permute-start | bytes 1105928 | tf_op jit(solution)/shard_map/ppermute | solution.py:17
  530.8 202.0 %collective-permute-start.3 = (bf16[1,1,720,256]{3,2,1,0:T(8,128)(2,1)S(1)}, bf16[1,1,720,256]{3,2,1,0:T(8,128)(2,1)S(1)}, u32[]{:S(2)}, u32[]{:S(2)}) collective-permute-start(bf16[1,1,720,256]{3,2,1,0:T(8,128)(2,1)S(1)} %get-tuple-element.235), channel_id=1, source_target_pairs={{64,0},{128,64},{192,128},{65,1},{129,65},{193,129},{66,2},{130,66... | collective-permute-start | bytes 1105928 | tf_op jit(solution)/shard_map/ppermute | solution.py:20
  732.9 1.3 copy-start.1
Sparse Core Ops, SparseCore 0:
  26.4 19.8 all-gather.3
  70.1 175.7 all-gather.5
  444.7 13.3 reduce-scatter.1
  464.0 265.1 all-reduce.3
where the time goes:
time: 742 us; the launch traced here: 741 us
  waiting for transfers between devices  399 us (54%)
  other arithmetic  159 us (21%)
  blocking collectives  73.8 us (10%)
  matrix products  59.5 us (8%)
  local copies, waits for them, and re-layouts  23.1 us (3%)
  between operations  15.1 us (2%)
  starting transfers between devices  12.1 us (2%)
    psum x1, waiting for transfers between devices, per_device(): weight_sum, loss = lax.psum((weight_part, loss_part), ('lat', 'lon', 'ens'))  195 us
    all_gather x1, waiting for transfers between devices, per_device(): ensemble = lax.all_gather(response, 'ens', axis=0, tiled=True)  174 us
    add x32, other arithmetic, add_member(): return (pair_dist + distance, pair_slope + gap_value / distance)  141 us
    psum x1, blocking collectives, per_device(): weight_sum, loss = lax.psum((weight_part, loss_part), ('lat', 'lon', 'ens'))  73.8 us
    all_gather x1, waiting for transfers between devices, per_device(): whole_circle = lax.all_gather(extended, 'lon', axis=2, tiled=True)  19.3 us
    dot_general x3, matrix products, per_device(): jnp.einsum('objq,eobjc->eoqc', kernels, picked, preferred_element_type=jn...  19.3 us
  transfers between devices with their start and end apart: 8, of which 5 were waited for; matrix products, arithmetic and copies ran while one was open for 2% of the time, Pallas kernels for 0%

commit v1 on v0

--- a/solution.py
+++ b/solution.py
@@ -3,10 +3,19 @@
 import jax.numpy as jnp
 from jax import lax
 from jax.sharding import PartitionSpec as P
+from jax.lax import psum
 
 PCAP = 2
 HMAX = 16
 highest = lax.Precision.HIGHEST
+
+
+def push_inputs(sheet):
+    axis_tag = "lat"
+    mesh_name = ("lon", "ens")
+    for idx in (mesh_name, axis_tag):
+        sheet = psum(sheet, idx)
+    return sheet
 
 
 def extended_2(block, sides, width):
@@ -129,7 +138,7 @@
     weight_part = jnp.einsum(
         "eokjc,eojd->kcd", features, slopes, preferred_element_type=jnp.float32
     )
-    weight_sum, loss = lax.psum((weight_part, loss_part), ("lat", "lon", "ens"))
+    weight_sum, loss = push_inputs((weight_part, loss_part))
     grad_weight = weight_sum * math.sqrt(weight.shape[0] * channels) / (lat_total * lon_total)
     feature_grad = jnp.einsum(
         "eojd,kcd->eokjc", slopes, weight, preferred_element_type=jnp.float32

time: 742 us -> 766 us (1.032); the launches traced: 741 us -> 755 us
  blocking collectives: 73.8 us -> 137 us
  waiting for transfers between devices: 399 us -> 349 us
    psum x1 -> x2, blocking collectives: 73.8 us -> 137 us  [push_inputs(): sheet = psum(sheet, idx)]
    psum x1 -> x2, waiting for transfers between devices: 195 us -> 143 us  [push_inputs(): sheet = psum(sheet, idx)]
  transfers between devices with their start and end apart: 8 -> 9, of which waited for: 5 -> 6; matrix products, arithmetic and copies ran while one was open for 2% -> 7% of each run, Pallas kernels for 0% -> 0%
where the time goes in v1:
time: 766 us; the launch traced here: 755 us
  waiting for transfers between devices  349 us (46%)
  other arithmetic  160 us (21%)
  blocking collectives  137 us (18%)
  matrix products  59.6 us (8%)
  local copies, waits for them, and re-layouts  22.2 us (3%)
  between operations  15.1 us (2%)
  starting transfers between devices  12.3 us (2%)
    all_gather x1, waiting for transfers between devices, per_device(): ensemble = lax.all_gather(response, 'ens', axis=0, tiled=True)  174 us
    psum x2, waiting for transfers between devices, push_inputs(): sheet = psum(sheet, idx)  143 us
    add x32, other arithmetic, add_member(): return (pair_dist + distance, pair_slope + gap_value / distance)  142 us
    psum x2, blocking collectives, push_inputs(): sheet = psum(sheet, idx)  137 us
    dot_general x3, matrix products, per_device(): jnp.einsum('objq,eobjc->eoqc', kernels, picked, preferred_element_type=jn...  19.3 us
    all_gather x1, waiting for transfers between devices, per_device(): whole_circle = lax.all_gather(extended, 'lon', axis=2, tiled=True)  19.3 us
  transfers between devices with their start and end apart: 9, of which 6 were waited for; matrix products, arithmetic and copies ran while one was open for 7% of the time, Pallas kernels for 0%

profile of v1, /device:TPU:2, one launch (start us, length us, event | category | flops | bytes accessed | tf_op | source)
XLA Modules:
  0.0 755.4 jit_solution(6883092710609126620)
XLA Ops:
  14.4 6.3 collective-permute-done
  27.0 19.3 %all-gather.4.cloned.1.call-done = bf16[1,4,1440,256]{3,2,1,0:T(8,128)(2,1)} async-done(((bf16[1,4,720,256]{3,2,1,0:T(8,128)(2,1)}), bf16[1,4,1440,256]{3,2,1,0:T(8,128)(2,1)}) %all-gather.4.cloned.1.call-update) | async-done | bytes 2949136 | tf_op jit(solution)/shard_map/all_gather | solution.py:105
  71.4 174.4 %all-gather.6.cloned.1.call-done = bf16[64,720,256]{2,1,0:T(8,128)(2,1)} async-done(((bf16[2,720,256]{2,1,0:T(8,128)(2,1)}), bf16[64,720,256]{2,1,0:T(8,128)(2,1)}) %all-gather.6.cloned.1.call-update) | async-done | bytes 23592976 | tf_op jit(solution)/shard_map/all_gather | solution.py:132
  245.8 142.3 %while.24 = (s32[]{:T(128)}, f32[1,2,720,256]{3,2,1,0:T(8,128)}, f32[1,2,720,256]{3,2,1,0:T(8,128)}, bf16[32,2,720,256]{3,2,1,0:T(8,128)(2,1)}, f32[1,2,720,256]{3,2,1,0:T(8,128)S(1)}, /*index=5*/s32[]{:T(128)}, s32[]{:T(128)}) while((s32[]{:T(128)}, f32[1,2,720,256]{3,2,1,0:T(8,128)}, f32[1,2,720,256]{3,2,1,0:T(8,128)}, ...), condition=%wide.region_1.2_spmd.clone, body=%wide.region_0.1_spmd.clone.sunk | while | flops 3317763 | bytes 8110179 | solution.py:83
  245.8 3.6 select_add_fusion.3
  249.5 4.5 select_add_fusion.3
  253.9 4.5 select_add_fusion.3
  258.4 4.5 select_add_fusion.3
  262.9 4.5 select_add_fusion.3
  267.4 4.5 select_add_fusion.3
  271.8 4.5 select_add_fusion.3
  276.3 4.5 select_add_fusion.3
  280.8 4.5 select_add_fusion.3
  285.3 4.5 select_add_fusion.3
  289.7 4.5 select_add_fusion.3
  294.2 4.5 select_add_fusion.3
  298.7 4.5 select_add_fusion.3
  303.2 4.5 select_add_fusion.3
  307.6 4.5 select_add_fusion.3
  312.1 4.5 select_add_fusion.3
  316.6 4.5 select_add_fusion.3
  321.0 4.5 select_add_fusion.3
  325.5 4.5 select_add_fusion.3
  330.0 4.5 select_add_fusion.3
  334.5 4.5 select_add_fusion.3
  338.9 4.5 select_add_fusion.3
  343.4 4.5 select_add_fusion.3
  347.9 4.5 select_add_fusion.3
  352.4 4.5 select_add_fusion.3
  356.8 4.5 select_add_fusion.3
  361.3 4.5 select_add_fusion.3
  365.8 4.5 select_add_fusion.3
  370.3 4.5 select_add_fusion.3
  374.7 4.5 select_add_fusion.3
  379.2 4.5 select_add_fusion.3
  383.7 4.5 select_add_fusion.3
  388.2 3.9 fusion.14
  392.1 6.4 convolution_bitcast_fusion.3
  398.4 3.9 fusion.1
  408.0 5.7 fusion.12
  415.5 6.8 fusion.11
  422.3 6.8 fusion.10
  429.4 5.4 broadcast_in_dim.38
  434.8 8.8 %dynamic_update_slice.3 = f32[1,4,2880,256]{3,2,1,0:T(8,128)} dynamic-update-slice(f32[1,4,2880,256]{3,2,1,0:T(8,128)} %broadcast_in_dim.38, f32[1,4,752,256]{3,2,1,0:T(8,128)} %fusion.10, s32[]{:T(128)} %constant.322.clone.1, s32[]{:T(128)} %constant.322.clone.1, s32[]{:T(128)S(6)} %select_n.39, s32[]{:T(128)} %constant.322.clone.1) | dynamic-update-slice | bytes 6160388 | tf_op jit(solution)/shard_map/dynamic_update_slice | solution.py:183
  443.6 9.5 %fusion.3 = bf16[1,4,1440,256]{3,2,1,0:T(8,128)(2,1)} fusion(f32[1,4,2880,256]{3,2,1,0:T(8,128)} %dynamic_update_slice.3, f32[3,4,256]{2,0,1:T(4,128)S(1)} %fusion.41, f32[1,1440]{1,0:T(1,128)S(1)} %copy-done.9, f32[1,1440]{1,0:T(1,128)S(1)} %copy-done.11, f32[3]{0:T(128)S(1)} %copy-done.13), kind=kOutput, calls=%fused_computation.12 | convolution fusion | flops 57516480 | bytes 14769420 | tf_op jit(solution)/shard_map/pj,eprc->erjc/dot_general | solution.py:181
  453.1 142.6 %all-reduce.5.cloned.1.call-done = f32[9,256,256]{2,1,0:T(8,128)} async-done(((f32[9,256,256]{2,1,0:T(8,128)}), f32[9,256,256]{2,1,0:T(8,128)}) %all-reduce.5.cloned.1.call-update) | async-done | bytes 2359312 | tf_op jit(solution)/shard_map/psum | solution.py:17
  596.4 128.1 %psum.30 = f32[]{:T(128)} all-reduce(f32[]{:T(128)S(6)} %div.141), channel_id=1, replica_groups=mesh['lat'=4,'lon'=2,'ens'=32] {'lon','ens'}, use_global_device_ids=true, to_apply=%region_9.10 | all-reduce | flops 1 | bytes 8 | tf_op jit(solution)/shard_map/psum | solution.py:17
  724.5 9.2 %psum.31 = f32[]{:T(128)} all-reduce(f32[]{:T(128)} %psum.30), channel_id=1, replica_groups=mesh['lat'=4,'lon'=2,'ens'=32] {'lat'}, use_global_device_ids=true, to_apply=%region_10.11 | all-reduce | flops 1 | bytes 8 | tf_op jit(solution)/shard_map/psum | solution.py:17
  (133 shorter events, 61.0 us)
Async XLA Ops:
  7.2 59.9 %copy-start = (bf16[9,256,256]{2,1,0:T(8,128)(2,1)S(1)}, bf16[9,256,256]{2,1,0:T(8,128)(2,1)}, u32[]{:S(2)}) copy-start(bf16[9,256,256]{2,1,0:T(8,128)(2,1)} %param.23) | copy-start | bytes 3538948
  7.2 19.2 %copy-start.14 = (s32[2]{0:T(128)S(1)}, s32[2]{0:T(128)}, u32[]{:S(2)}) copy-start(s32[2]{0:T(128)} %param.24) | copy-start | bytes 28
  7.2 39.0 %all-gather.4.cloned.1.call-start = ((), (), s32[]{:S(2)}) async-start(), calls=%async_computation.1 | async-start | bytes 4423680 | tf_op jit(solution)/shard_map/all_gather | solution.py:105
  8.5 12.2 %collective-permute-start = (bf16[1,1,720,256]{3,2,1,0:T(8,128)(2,1)S(1)}, bf16[1,1,720,256]{3,2,1,0:T(8,128)(2,1)S(1)}, u32[]{:S(2)}, u32[]{:S(2)}) collective-permute-start(bf16[1,1,720,256]{3,2,1,0:T(8,128)(2,1)S(1)} %get-tuple-element.236), channel_id=1, source_target_pairs={{0,64},{64,128},{128,192},{1,65},{65,129},{129,193},{2,66},{66,130... | collective-permute-start | bytes 1105928 | tf_op jit(solution)/shard_map/ppermute | solution.py:26
  11.9 11.9 %collective-permute-start.1 = (bf16[1,1,720,256]{3,2,1,0:T(8,128)(2,1)S(1)}, bf16[1,1,720,256]{3,2,1,0:T(8,128)(2,1)S(1)}, u32[]{:S(2)}, u32[]{:S(2)}) collective-permute-start(bf16[1,1,720,256]{3,2,1,0:T(8,128)(2,1)S(1)} %get-tuple-element.237), channel_id=1, source_target_pairs={{64,0},{128,64},{192,128},{65,1},{129,65},{193,129},{66,2},{130,66... | collective-permute-start | bytes 1105928 | tf_op jit(solution)/shard_map/ppermute | solution.py:29
  26.2 219.6 %all-gather.6.cloned.1.call-start = ((), (), s32[]{:S(2)}) async-start(), calls=%async_computation.5 | async-start | bytes 24330240 | tf_op jit(solution)/shard_map/all_gather | solution.py:132
  26.3 25.0 %copy-start.12 = (f32[3]{0:T(128)}, f32[3]{0:T(128)S(1)}, u32[]{:S(2)}) copy-start(f32[3]{0:T(128)S(1)} %pad.37.clone) | copy-start | bytes 40
  26.7 24.6 %copy-start.8 = (f32[1,1440]{1,0:T(1,128)}, f32[1,1440]{1,0:T(1,128)S(1)}, u32[]{:S(2)}) copy-start(f32[1,1440]{1,0:T(1,128)S(1)} %get-tuple-element.247) | copy-start | bytes 17284
  26.7 24.6 %copy-start.10 = (f32[1,1440]{1,0:T(1,128)}, f32[1,1440]{1,0:T(1,128)S(1)}, u32[]{:S(2)}) copy-start(f32[1,1440]{1,0:T(1,128)S(1)} %get-tuple-element.248) | copy-start | bytes 17284
  26.9 30.9 %copy-start.6 = (f32[720,752]{1,0:T(8,128)}, f32[720,752]{1,0:T(8,128)S(1)}, u32[]{:S(2)}) copy-start(f32[720,752]{1,0:T(8,128)S(1)} %subtract_convert_fusion) | copy-start | bytes 6497284
  46.2 3.3 copy-start.2
  64.3 2.8 copy-start.4
  69.9 525.9 %all-reduce.5.cloned.1.call-start = ((), (), s32[]{:S(2)}) async-start(), calls=%async_computation.3 | async-start | bytes 4718592 | tf_op jit(solution)/shard_map/psum | solution.py:17
  245.8 142.3 %copy-start.5 = (bf16[2,720,256]{2,1,0:T(8,128)(2,1)S(1)}, bf16[2,720,256]{2,1,0:T(8,128)(2,1)}, u32[]{:S(2)}) copy-start(bf16[2,720,256]{2,1,0:T(8,128)(2,1)} %bitcast_convert_fusion) | copy-start | bytes 2211844
  406.3 1.6 copy-start.7
  407.5 326.2 %reduce-scatter.2.cloned.1.call-start = ((), (), s32[]{:S(2)}) async-start(), calls=%async_computation.2 | async-start | bytes 4423680 | tf_op jit(solution)/shard_map/reduce_scatter | solution.py:185
  434.8 8.8 %copy-start.9 = (f32[1,1440]{1,0:T(1,128)S(1)}, f32[1,1440]{1,0:T(1,128)}, u32[]{:S(2)}) copy-start(f32[1,1440]{1,0:T(1,128)} %copy-done.8) | copy-start | bytes 17284
  434.8 8.8 %copy-start.11 = (f32[1,1440]{1,0:T(1,128)S(1)}, f32[1,1440]{1,0:T(1,128)}, u32[]{:S(2)}) copy-start(f32[1,1440]{1,0:T(1,128)} %copy-done.10) | copy-start | bytes 17284
  434.8 8.8 %copy-start.13 = (f32[3]{0:T(128)S(1)}, f32[3]{0:T(128)}, u32[]{:S(2)}) copy-start(f32[3]{0:T(128)} %copy-done.12) | copy-start | bytes 40
  453.1 287.8 %all-reduce.7.cloned.1.call-start = ((), (), s32[]{:S(2)}) async-start(), calls=%async_computation.4 | async-start | bytes 4718592 | tf_op jit(solution)/shard_map/psum | solution.py:17
  733.7 10.4 %copy-start.3 = (bf16[1,4,720,256]{3,2,1,0:T(8,128)(2,1)S(1)}, bf16[1,4,720,256]{3,2,1,0:T(8,128)(2,1)}, u32[]{:S(2)}) copy-start(bf16[1,4,720,256]{3,2,1,0:T(8,128)(2,1)} %reduce-scatter.2.cloned.1.call-done) | copy-start | bytes 4423684
  735.0 9.6 %collective-permute-start.2 = (bf16[1,1,720,256]{3,2,1,0:T(8,128)(2,1)S(1)}, bf16[1,1,720,256]{3,2,1,0:T(8,128)(2,1)S(1)}, u32[]{:S(2)}, u32[]{:S(2)}) collective-permute-start(bf16[1,1,720,256]{3,2,1,0:T(8,128)(2,1)S(1)} %get-tuple-element.234), channel_id=1, source_target_pairs={{0,64},{64,128},{128,192},{1,65},{65,129},{129,193},{2,66},{66,130... | collective-permute-start | bytes 1105928 | tf_op jit(solution)/shard_map/ppermute | solution.py:26
  738.1 9.4 %collective-permute-start.3 = (bf16[1,1,720,256]{3,2,1,0:T(8,128)(2,1)S(1)}, bf16[1,1,720,256]{3,2,1,0:T(8,128)(2,1)S(1)}, u32[]{:S(2)}, u32[]{:S(2)}) collective-permute-start(bf16[1,1,720,256]{3,2,1,0:T(8,128)(2,1)S(1)} %get-tuple-element.235), channel_id=1, source_target_pairs={{64,0},{128,64},{192,128},{65,1},{129,65},{193,129},{66,2},{130,66... | collective-permute-start | bytes 1105928 | tf_op jit(solution)/shard_map/ppermute | solution.py:29
  747.5 1.4 copy-start.1
Sparse Core Ops, SparseCore 0:
  26.4 19.8 all-gather.3
  70.0 175.7 all-gather.5
  407.6 188.1 all-reduce.4
  598.1 15.0 reduce-scatter.1
  615.4 68.1 all-reduce.6
